TPU v7x, 256 devices: a whole 4x4x8 slice. The times are simulated.
256 devices in a mesh: row: 32 (over z_lo, x, core), col: 8 (over z_hi, y).
Axes of the slice: x: 4, y: 4, z: 8 (z_hi: 2, z_lo: 4; z = z_hi * 4 + z_lo), core: 2. Of those that a mesh axis runs over, the one named last changes fastest.
Arguments:
- ancestors: bfloat16 [128, 128, 256, 256], P('row', 'col'), may hold values from -6 to 6
- panel_one: bfloat16 [2, 128, 256, 256], P(None, 'row'), may hold values from -0.0625 to 0.0625
- present_one: int32 [2, 128], replicated, may hold values from 0 to 1, as said below
- dinv_one: bfloat16 [2, 256, 256], replicated, may hold values from -6 to 6
- panel_two: bfloat16 [2, 128, 256, 256], P(None, 'row'), may hold values from -0.0625 to 0.0625
- present_two: int32 [2, 128], replicated, may hold values from 0 to 1, as said below
- dinv_two: bfloat16 [2, 256, 256], replicated, may hold values from -6 to 6
Outputs:
- update_one: float32 [256, 256, 256], P(('row', 'col'))
- diag_one: float32 [2, 256, 256], replicated
- update_two: float32 [256, 256, 256], P(('row', 'col'))
- diag_two: float32 [2, 256, 256], replicated
Inputs may be any that keep to these rules, and one draw needn't show every extreme that they name: `present_one`: each supernode's row has 16 to 64 ones, block row 0 among them; the first supernode of each level has exactly 64. `present_two`: each supernode's row has 16 to 64 ones, block row 0 among them; the first supernode of each level has exactly 64.
All inputs are finite; a program needn't handle non-finite values.
Results may differ from a plain program's by a relative error of at most 0.0003.
Values may be sent and summed in bfloat16 or wider, within the bound.
No kernel may reach another device: no remote copies, remote signals or barrier semaphores. Data moves between devices by JAX's collectives and lax.ppermute only.
A program may use at most 128 MiB of HBM per device.

v0:
```python
import jax
import jax.numpy as jnp
from jax import lax
from jax.sharding import PartitionSpec as P


def spread(block, axis, holder):
    block = jnp.where(lax.axis_index(axis) == holder, block, jnp.zeros_like(block))
    return lax.psum(block, axis)


def one_level(ancestors, panel_part, present, inv_diag):
    a_row = ancestors.shape[0]
    a_col = ancestors.shape[1]
    block_size = ancestors.shape[2]
    count_s = panel_part.shape[0]
    row_at = lax.axis_index("row")
    col_at = lax.axis_index("col")
    root_count = a_col // a_row
    pieces = []
    for offset in range(root_count):
        pieces.append(spread(panel_part, "row", col_at * root_count + offset))
    column_panel = jnp.concatenate(pieces, axis=1)
    col_mask = lax.dynamic_slice_in_dim(present, col_at * a_col, a_col, 1)
    row_mask = lax.dynamic_slice_in_dim(present, row_at * a_row, a_row, 1)
    masked = column_panel * col_mask[:, :, None, None].astype(jnp.bfloat16)
    partial_sums = jnp.einsum(
        "ijab,kjbc->ikac", ancestors, masked, preferred_element_type=jnp.float32
    )
    term_blocks = -partial_sums * jnp.transpose(row_mask).astype(jnp.float32)[:, :, None, None]
    flat_terms = term_blocks.reshape(a_row * count_s, block_size, block_size)
    owned_blocks = lax.psum_scatter(flat_terms, "col", scatter_dimension=0, tiled=True)
    panel_flat = jnp.transpose(panel_part, (1, 0, 2, 3)).reshape(
        a_row * count_s, block_size, block_size
    )
    owned_count = owned_blocks.shape[0]
    first_row = col_at * owned_count
    panel_own = lax.dynamic_slice_in_dim(panel_flat, first_row, owned_count, 0)
    products = jnp.einsum(
        "nba,nbc->nac", panel_own.astype(jnp.float32), owned_blocks, precision=lax.Precision.HIGHEST
    )
    sup_index = (first_row + jnp.arange(owned_count, dtype=jnp.int32)) % count_s
    one_hot_rows = (sup_index[:, None] == jnp.arange(count_s, dtype=jnp.int32)[None, :]).astype(
        jnp.float32
    )
    diag_terms = jnp.einsum("nk,nac->kac", one_hot_rows, products, precision=lax.Precision.HIGHEST)
    diag_total = lax.psum(diag_terms, ("row", "col"))
    return (owned_blocks, inv_diag.astype(jnp.float32) - diag_total)


def body(ancestors, panel_one, present_one, dinv_one, panel_two, present_two, dinv_two):
    update_one, diag_one = one_level(ancestors, panel_one, present_one, dinv_one)
    update_two, diag_two = one_level(ancestors, panel_two, present_two, dinv_two)
    return (update_one, diag_one, update_two, diag_two)


def solution(mesh):
    in_specs = (
        P("row", "col", None, None),
        P(None, "row", None, None),
        P(),
        P(),
        P(None, "row", None, None),
        P(),
        P(),
    )
    out_specs = (P(("row", "col"), None, None), P(), P(("row", "col"), None, None), P())
    return jax.shard_map(body, mesh=mesh, in_specs=in_specs, out_specs=out_specs, check_vma=False)
```

profile of v0, /device:TPU:2, one launch (start us, length us, event | category | flops | bytes accessed | tf_op | source)
XLA Modules:
  0.0 787.7 jit_solution(2082607152326001342)
XLA Ops:
  7.2 0.0 all-reduce.7.cloned.1.call-start
  7.2 4.8 broadcast_select_fusion.6
  12.0 0.0 copy-start.4
  12.0 0.0 copy-start.5
  12.1 0.0 all-reduce.7.cloned.1.call-update
  12.1 0.0 reduce-scatter.5.cloned.1.call-start
  12.1 0.6 copy-done.4
  12.7 0.0 copy-done.5
  12.7 0.1 fusion.40
  12.8 0.1 fusion.42
  12.9 299.0 %all-reduce.7.cloned.1.call-done = (bf16[2,4,256,256]{3,2,1,0:T(8,128)(2,1)}, bf16[2,4,256,256]{3,2,1,0:T(8,128)(2,1)}, bf16[2,4,256,256]{3,2,1,0:T(8,128)(2,1)}...) async-done(((bf16[2,4,256,256]{3,2,1,0:T(8,128)(2,1)}, ...) | async-done | bytes 8388624 | tf_op jit(solution)/shard_map/psum | solution.py:9
  311.9 10.0 %bitcast_multiply_fusion = f32[4,2,256,256]{2,3,0,1:T(8,128)S(1)} fusion(bf16[4,16,256,256]{3,2,1,0:T(8,128)(2,1)} %param.7, bf16[2,4,256,256]{3,2,1,0:T(8,128)(2,1)} %get-tuple-element.10, bf16[2,4,256,256]{3,2,1,0:T(8,128)(2,1)} %get-tuple-element.11, bf16[2,4,256,256]{3,2,1,0:T(8,128)(2,1)} %get-tuple-element.12, ...), kind=kOutput, calls=%fused_computation.20 | convolution fusion | flops 4316987392 | bytes 14680160 | tf_op jit(solution)/shard_map/ijab,kjbc->ikac/dot_general | solution.py:27
  321.9 0.0 copy-start.6
  321.9 1.8 copy.17
  323.7 0.0 reduce-scatter.5.cloned.1.call-update
  323.8 0.0 reduce-scatter.3.cloned.1.call-start
  323.8 0.0 copy-done.6
  323.8 11.3 %bitcast_multiply_fusion.1 = f32[4,2,256,256]{2,3,0,1:T(8,128)} fusion(bf16[4,16,256,256]{3,2,1,0:T(8,128)(2,1)} %param.7, bf16[2,4,256,256]{3,2,1,0:T(8,128)(2,1)S(1)} %copy-done.6, bf16[2,4,256,256]{3,2,1,0:T(8,128)(2,1)} %get-tuple-element.7, bf16[2,4,256,256]{3,2,1,0:T(8,128)(2,1)} %get-tuple-element.8, bf16[2,4,256,256]{3,2,1,0:T(8,128)(2,1)} %get-tuple-element.9, ...), kind=kOutput, calls=%fused_computation.22 | convolution fusion | flops 4316987392 | bytes 14680160 | tf_op jit(solution)/shard_map/ijab,kjbc->ikac/dot_general | solution.py:27
  335.2 0.0 copy-start
  335.2 0.0 copy-start.1
  335.2 3.1 copy.14
  338.2 0.0 reduce-scatter.3.cloned.1.call-update
  338.3 0.0 copy-start.2
  338.3 0.0 all-reduce.5.cloned.1.call-start
  338.3 0.0 copy-done
  338.3 0.1 copy.18
  338.4 0.0 copy-done.1
  338.4 0.1 copy.15
  338.5 0.0 copy-start.3
  338.5 84.9 %reduce-scatter.5.cloned.1.call-done = f32[1,256,256]{2,1,0:T(8,128)} async-done(((f32[8,256,256]{2,1,0:T(8,128)}), f32[1,256,256]{2,1,0:T(8,128)}) %reduce-scatter.5.cloned.1.call-update) | async-done | bytes 262160 | tf_op jit(solution)/shard_map/reduce_scatter | solution.py:32
  423.4 1.3 fusion.30
  424.7 94.8 %reduce-scatter.3.cloned.1.call-done = f32[1,256,256]{2,1,0:T(8,128)} async-done(((f32[8,256,256]{2,1,0:T(8,128)}), f32[1,256,256]{2,1,0:T(8,128)}) %reduce-scatter.3.cloned.1.call-update) | async-done | bytes 262160 | tf_op jit(solution)/shard_map/reduce_scatter | solution.py:32
  519.5 1.3 fusion.32
  520.7 1.1 broadcast_multiply_fusion
  521.8 0.0 all-reduce.5.cloned.1.call-update
  521.9 255.5 %all-reduce.5.cloned.1.call-done = (f32[2,256,256]{2,1,0:T(8,128)}, f32[2,256,256]{2,1,0:T(8,128)}) async-done(((f32[2,256,256]{2,1,0:T(8,128)}, f32[2,256,256]{2,1,0:T(8,128)}), (f32[2,256,256]{2,1,0:T(8,128)}, f32[2,256,256]{2,1,0:T(8,128)})) %all-reduce.5.cloned.1.call-update) | async-done | bytes 1048592 | tf_op jit(solution)/shard_map/psum | solution.py:47
  777.4 0.0 copy-done.2
  777.4 1.9 convert_subtract_fusion
  779.3 0.0 copy-done.3
  779.3 1.9 convert_subtract_fusion.1
  (1 shorter events, 0.0 us)
Async XLA Ops:
  7.2 304.7 %all-reduce.7.cloned.1.call-start = ((), (), s32[]{:S(2)}) async-start(), calls=%async_computation.5 | async-start | bytes 16777216 | tf_op jit(solution)/shard_map/psum | solution.py:9
  12.0 0.7 copy-start.4
  12.0 0.7 copy-start.5
  12.1 411.3 %reduce-scatter.5.cloned.1.call-start = ((), (), s32[]{:S(2)}) async-start(), calls=%async_computation.3 | async-start | bytes 2359296 | tf_op jit(solution)/shard_map/reduce_scatter | solution.py:32
  321.9 1.9 copy-start.6
  323.8 195.7 %reduce-scatter.3.cloned.1.call-start = ((), (), s32[]{:S(2)}) async-start(), calls=%async_computation.2 | async-start | bytes 2359296 | tf_op jit(solution)/shard_map/reduce_scatter | solution.py:32
  335.2 3.2 copy-start
  335.2 3.2 copy-start.1
  338.3 439.1 %copy-start.2 = (bf16[2,256,256]{2,1,0:T(8,128)(2,1)S(1)}, bf16[2,256,256]{2,1,0:T(8,128)(2,1)}, u32[]{:S(2)}) copy-start(bf16[2,256,256]{2,1,0:T(8,128)(2,1)} %param.13) | copy-start | bytes 786436
  338.3 439.1 %all-reduce.5.cloned.1.call-start = ((), (), s32[]{:S(2)}) async-start(), calls=%async_computation.4 | async-start | bytes 2097152 | tf_op jit(solution)/shard_map/psum | solution.py:47
  338.5 440.8 %copy-start.3 = (bf16[2,256,256]{2,1,0:T(8,128)(2,1)S(1)}, bf16[2,256,256]{2,1,0:T(8,128)(2,1)}, u32[]{:S(2)}) copy-start(bf16[2,256,256]{2,1,0:T(8,128)(2,1)} %param.10) | copy-start | bytes 786436
Sparse Core Ops, SparseCore 0:
  12.2 299.6 all-reduce.6
  323.9 99.4 reduce-scatter.4
  428.6 90.8 reduce-scatter.2
  525.5 251.8 all-reduce.4
where the time goes:
time: 788 us
  waiting for transfers between devices  734 us (93%)
  matrix products  23.8 us (3%)
  between operations  13.9 us (2%)
  other arithmetic  9.86 us (1%)
    psum x1, waiting for transfers between devices, spread(): return lax.psum(block, axis)  299 us
    psum x1, waiting for transfers between devices, one_level(): diag_total = lax.psum(diag_terms, ('row', 'col'))  256 us
    reduce_scatter x2, waiting for transfers between devices, one_level(): lax.psum_scatter(flat_terms, 'col', scatter_dimension=0, tiled=True)  180 us
    dot_general x2, matrix products, one_level(): jnp.einsum('ijab,kjbc->ikac', ancestors, masked, preferred_element_type=j...  21.3 us
  transfers between devices with their start and end apart: 4, of which 4 were waited for; matrix products, arithmetic and copies ran while one was open for 2% of the time, Pallas kernels for 0%

commit v1 on v0

--- a/solution.py
+++ b/solution.py
@@ -44,7 +44,7 @@
         jnp.float32
     )
     diag_terms = jnp.einsum("nk,nac->kac", one_hot_rows, products, precision=lax.Precision.HIGHEST)
-    diag_total = lax.psum(diag_terms, ("row", "col"))
+    diag_total = lax.psum(lax.psum(diag_terms, "row"), "col")
     return (owned_blocks, inv_diag.astype(jnp.float32) - diag_total)
 
 

time: 788 us -> 922 us (1.17)
  waiting for transfers between devices: 734 us -> 868 us
    psum x1 -> x2, waiting for transfers between devices: 256 us -> 389 us  [one_level(): diag_total = lax.psum(lax.psum(diag_terms, 'row'), 'col')]
  transfers between devices with their start and end apart: 4 -> 5, of which waited for: 4 -> 5; matrix products, arithmetic and copies ran while one was open for 2% -> 2% of each run, Pallas kernels for 0% -> 0%
where the time goes in v1:
time: 922 us; the launch traced here: 921 us
  waiting for transfers between devices  868 us (94%)
  matrix products  23.8 us (3%)
  between operations  13.9 us (2%)
  other arithmetic  9.85 us (1%)
    psum x2, waiting for transfers between devices, one_level(): diag_total = lax.psum(lax.psum(diag_terms, 'row'), 'col')  389 us
    psum x1, waiting for transfers between devices, spread(): return lax.psum(block, axis)  299 us
    reduce_scatter x2, waiting for transfers between devices, one_level(): lax.psum_scatter(flat_terms, 'col', scatter_dimension=0, tiled=True)  180 us
    dot_general x2, matrix products, one_level(): jnp.einsum('ijab,kjbc->ikac', ancestors, masked, preferred_element_type=j...  21.3 us
  transfers between devices with their start and end apart: 5, of which 5 were waited for; matrix products, arithmetic and copies ran while one was open for 2% of the time, Pallas kernels for 0%

profile of v1, /device:TPU:2, one launch (start us, length us, event | category | flops | bytes accessed | tf_op | source)
XLA Modules:
  0.0 921.4 jit_solution(11884126976590032399)
XLA Ops:
  7.2 0.0 all-reduce.11.cloned.1.call-start
  7.2 4.8 broadcast_select_fusion.6
  12.0 0.0 copy-start.4
  12.0 0.0 copy-start.5
  12.0 0.0 all-reduce.11.cloned.1.call-update
  12.1 0.0 reduce-scatter.5.cloned.1.call-start
  12.1 0.6 copy-done.4
  12.7 0.0 copy-done.5
  12.7 0.1 fusion.40
  12.8 0.1 fusion.42
  12.9 299.0 %all-reduce.11.cloned.1.call-done = (bf16[2,4,256,256]{3,2,1,0:T(8,128)(2,1)}, bf16[2,4,256,256]{3,2,1,0:T(8,128)(2,1)}, bf16[2,4,256,256]{3,2,1,0:T(8,128)(2,1)...) async-done(((bf16[2,4,256,256]{3,2,1,0:T(8,128)(2,1)}, ...) | async-done | bytes 8388624 | tf_op jit(solution)/shard_map/psum | solution.py:9
  311.9 10.0 %bitcast_multiply_fusion = f32[4,2,256,256]{2,3,0,1:T(8,128)S(1)} fusion(bf16[4,16,256,256]{3,2,1,0:T(8,128)(2,1)} %param.7, bf16[2,4,256,256]{3,2,1,0:T(8,128)(2,1)} %get-tuple-element.12, bf16[2,4,256,256]{3,2,1,0:T(8,128)(2,1)} %get-tuple-element.13, bf16[2,4,256,256]{3,2,1,0:T(8,128)(2,1)} %get-tuple-element.14, ...), kind=kOutput, calls=%fused_computation.20 | convolution fusion | flops 4316987392 | bytes 14680160 | tf_op jit(solution)/shard_map/ijab,kjbc->ikac/dot_general | solution.py:27
  321.9 0.0 copy-start.6
  321.9 1.8 copy.17
  323.7 0.0 reduce-scatter.5.cloned.1.call-update
  323.8 0.0 reduce-scatter.3.cloned.1.call-start
  323.8 0.0 copy-done.6
  323.8 11.4 %bitcast_multiply_fusion.1 = f32[4,2,256,256]{2,3,0,1:T(8,128)} fusion(bf16[4,16,256,256]{3,2,1,0:T(8,128)(2,1)} %param.7, bf16[2,4,256,256]{3,2,1,0:T(8,128)(2,1)S(1)} %copy-done.6, bf16[2,4,256,256]{3,2,1,0:T(8,128)(2,1)} %get-tuple-element.9, bf16[2,4,256,256]{3,2,1,0:T(8,128)(2,1)} %get-tuple-element.10, ...), kind=kOutput, calls=%fused_computation.22 | convolution fusion | flops 4316987392 | bytes 14680160 | tf_op jit(solution)/shard_map/ijab,kjbc->ikac/dot_general | solution.py:27
  335.2 0.0 copy-start
  335.2 0.0 copy-start.1
  335.2 3.1 copy.14
  338.2 0.0 reduce-scatter.3.cloned.1.call-update
  338.3 0.0 all-reduce.7.cloned.1.call-start
  338.3 0.0 copy-done
  338.3 0.0 copy-start.2
  338.3 0.1 copy.18
  338.4 0.0 copy-done.1
  338.4 0.1 copy.15
  338.5 0.0 copy-start.3
  338.5 84.9 %reduce-scatter.5.cloned.1.call-done = f32[1,256,256]{2,1,0:T(8,128)} async-done(((f32[8,256,256]{2,1,0:T(8,128)}), f32[1,256,256]{2,1,0:T(8,128)}) %reduce-scatter.5.cloned.1.call-update) | async-done | bytes 262160 | tf_op jit(solution)/shard_map/reduce_scatter | solution.py:32
  423.5 1.3 fusion.30
  424.7 94.8 %reduce-scatter.3.cloned.1.call-done = f32[1,256,256]{2,1,0:T(8,128)} async-done(((f32[8,256,256]{2,1,0:T(8,128)}), f32[1,256,256]{2,1,0:T(8,128)}) %reduce-scatter.3.cloned.1.call-update) | async-done | bytes 262160 | tf_op jit(solution)/shard_map/reduce_scatter | solution.py:32
  519.6 1.3 fusion.32
  520.8 1.1 broadcast_multiply_fusion
  522.0 0.0 all-reduce.7.cloned.1.call-update
  522.0 0.0 all-reduce.9.cloned.1.call-start
  522.0 269.4 %all-reduce.7.cloned.1.call-done = (f32[2,256,256]{2,1,0:T(8,128)}, f32[2,256,256]{2,1,0:T(8,128)}) async-done(((f32[2,256,256]{2,1,0:T(8,128)}, f32[2,256,256]{2,1,0:T(8,128)}), (f32[2,256,256]{2,1,0:T(8,128)}, f32[2,256,256]{2,1,0:T(8,128)})) %all-reduce.7.cloned.1.call-update) | async-done | bytes 1048592 | tf_op jit(solution)/shard_map/psum | solution.py:47
  791.5 0.0 all-reduce.9.cloned.1.call-update
  791.5 119.6 %all-reduce.9.cloned.1.call-done = (f32[2,256,256]{2,1,0:T(8,128)}, f32[2,256,256]{2,1,0:T(8,128)}) async-done(((f32[2,256,256]{2,1,0:T(8,128)}, f32[2,256,256]{2,1,0:T(8,128)}), (f32[2,256,256]{2,1,0:T(8,128)}, f32[2,256,256]{2,1,0:T(8,128)})) %all-reduce.9.cloned.1.call-update) | async-done | bytes 1048592 | tf_op jit(solution)/shard_map/psum | solution.py:47
  911.1 0.0 copy-done.2
  911.1 1.9 convert_subtract_fusion
  913.0 0.0 copy-done.3
  913.0 1.9 convert_subtract_fusion.1
  (1 shorter events, 0.0 us)
Async XLA Ops:
  7.2 304.7 %all-reduce.11.cloned.1.call-start = ((), (), s32[]{:S(2)}) async-start(), calls=%async_computation.6 | async-start | bytes 16777216 | tf_op jit(solution)/shard_map/psum | solution.py:9
  12.0 0.7 copy-start.4
  12.0 0.7 copy-start.5
  12.1 411.4 %reduce-scatter.5.cloned.1.call-start = ((), (), s32[]{:S(2)}) async-start(), calls=%async_computation.3 | async-start | bytes 2359296 | tf_op jit(solution)/shard_map/reduce_scatter | solution.py:32
  321.9 1.9 copy-start.6
  323.8 195.8 %reduce-scatter.3.cloned.1.call-start = ((), (), s32[]{:S(2)}) async-start(), calls=%async_computation.2 | async-start | bytes 2359296 | tf_op jit(solution)/shard_map/reduce_scatter | solution.py:32
  335.2 3.2 copy-start
  335.2 3.3 copy-start.1
  338.3 453.2 %all-reduce.7.cloned.1.call-start = ((), (), s32[]{:S(2)}) async-start(), calls=%async_computation.4 | async-start | bytes 2097152 | tf_op jit(solution)/shard_map/psum | solution.py:47
  338.3 572.8 %copy-start.2 = (bf16[2,256,256]{2,1,0:T(8,128)(2,1)S(1)}, bf16[2,256,256]{2,1,0:T(8,128)(2,1)}, u32[]{:S(2)}) copy-start(bf16[2,256,256]{2,1,0:T(8,128)(2,1)} %param.13) | copy-start | bytes 786436
  338.5 574.5 %copy-start.3 = (bf16[2,256,256]{2,1,0:T(8,128)(2,1)S(1)}, bf16[2,256,256]{2,1,0:T(8,128)(2,1)}, u32[]{:S(2)}) copy-start(bf16[2,256,256]{2,1,0:T(8,128)(2,1)} %param.10) | copy-start | bytes 786436
  522.0 389.2 %all-reduce.9.cloned.1.call-start = ((), (), s32[]{:S(2)}) async-start(), calls=%async_computation.5 | async-start | bytes 2097152 | tf_op jit(solution)/shard_map/psum | solution.py:47
Sparse Core Ops, SparseCore 0:
  12.2 299.6 all-reduce.10
  323.9 99.5 reduce-scatter.4
  428.7 90.8 reduce-scatter.2
  522.6 268.7 all-reduce.6
  794.2 116.8 all-reduce.8
